TPU v7x, 128 devices: a whole 4x4x4 slice. The times are simulated.
128 devices in a mesh: wide: 16 (over y, z), narrow: 8 (over x, core).
Axes of the slice: x: 4, y: 4, z: 4, core: 2. Of those that a mesh axis runs over, the one named last changes fastest.
Arguments:
- hidden: bfloat16 [128, 16384], P('narrow', 'wide'), may hold values from -6 to 6
- gain: bfloat16 [16384], P('wide'), may hold values from 0.5 to 1.5
- sign_in: int32 [16384], P('wide'), may hold values from 0 to 1
- qkv_weight: bfloat16 [16384, 18432], P('wide', 'narrow'), may hold values from -0.046875 to 0.046875
- out_weight: bfloat16 [16384, 16384], P('narrow', 'wide'), may hold values from -0.046875 to 0.046875
- sign_attn: int32 [16384], P('narrow'), may hold values from 0 to 1
- key_cache: bfloat16 [128, 8, 4096, 128], P('wide', 'narrow'), may hold values from -512 to 512, as said below
- value_cache: bfloat16 [128, 8, 4096, 128], P('wide', 'narrow'), may hold values from -6 to 6
- lengths: int32 [128], P('wide'), may hold values from 1024 to 4096
Outputs:
- layer_out: bfloat16 [128, 16384], P('narrow', 'wide')
Inputs may be any that keep to these rules, and one draw needn't show every extreme that they name: `key_cache`: cached keys mostly of magnitude about 2, with some slots far larger in the hidden draw.
All inputs are finite; a program needn't handle non-finite values. Where the computation divides by a largest or mean magnitude, that divisor is 1e-20 or more.
Results may differ from a plain program's by a relative error of at most 0.018.
Values may be sent and summed in bfloat16 or wider, within the bound.
No kernel may reach another device: no remote copies, remote signals or barrier semaphores. Data moves between devices by JAX's collectives and lax.ppermute only.
A program may use at most 128 MiB of HBM per device.

v0:
```python
import math
import jax
import jax.numpy as jnp
from jax import lax
from jax.sharding import Mesh
from jax.sharding import PartitionSpec as P

D = 16384
HD = 128
QG = 16
WIDE = ("wide_0", "wide_1")
ROPE_BASE = 500000.0


def one_axis_at_a_time(value, axes):
    for axis in axes:
        value = lax.psum(value, axis)
    return value


def side_by_side(arrays, axis, dim, along):
    columns = [a.reshape(*a.shape[:along], -1) for a in arrays]
    both = jnp.concatenate(columns, axis=along)
    filled, at, gathered = (lax.all_gather(both, axis, axis=dim, tiled=True), 0, [])
    for a, column in zip(arrays, columns):
        piece = filled[..., at : at + column.shape[along]]
        gathered.append(piece.reshape(*piece.shape[:along], *a.shape[along:]))
        at += column.shape[along]
    return tuple(gathered)


def split_up(value, dim, peers):
    before, after = (value.shape[:dim], value.shape[dim + 1 :])
    return jnp.moveaxis(value.reshape(*before, peers, -1, *after), dim, 0)


def summed_on_arrival(value, axis, dim):
    tiles = split_up(value, dim, lax.axis_size(axis))
    arrived = lax.all_to_all(tiles, axis, split_axis=0, concat_axis=0, tiled=True)
    return arrived.astype(jnp.float32).sum(axis=0)


def hadamard(order):
    places = jnp.arange(order, dtype=jnp.int32)
    common = places[:, None] & places[None, :]
    parity = jnp.zeros((order, order), jnp.int32)
    for bit_pos in range(order.bit_length() - 1):
        parity = parity ^ common >> bit_pos & 1
    return (1 - 2 * parity).astype(jnp.float32) / math.sqrt(order)


def rotate_blocks(values, sign_bits, width):
    signs = (2 * sign_bits - 1).astype(jnp.float32)
    blocks = (values * signs).reshape(values.shape[:-1] + (values.shape[-1] // width, width))
    turned = jnp.einsum("...bk,kj->...bj", blocks, hadamard(width))
    scales = (jnp.max(jnp.abs(turned), axis=-1) + 1e-06).astype(jnp.bfloat16)
    payload = (turned / scales.astype(jnp.float32)[..., None]).astype(jnp.bfloat16)
    return (payload, scales)


def rotary(vectors, positions):
    half_width = vectors.shape[-1] // 2
    frequency = jnp.exp(
        jnp.arange(half_width, dtype=jnp.float32) * (-2.0 * math.log(ROPE_BASE) / vectors.shape[-1])
    )
    angles = positions.astype(jnp.float32)[:, None] * frequency[None, :]
    cosine = jnp.cos(angles)[:, None, :]
    sines = jnp.sin(angles)[:, None, :]
    lower_half = vectors[..., :half_width]
    upper_half = vectors[..., half_width:]
    return jnp.concatenate(
        [lower_half * cosine - upper_half * sines, upper_half * cosine + lower_half * sines],
        axis=-1,
    )


def body(hidden, gain, sign_in, qkv_weight, out_weight, sign_attn, key_cache, value_cache, lengths):
    rows = hidden.astype(jnp.float32)
    squares = one_axis_at_a_time(jnp.sum(rows * rows, axis=1), WIDE)
    factor = lax.rsqrt(squares / D + 1e-05)
    normed = rows * factor[:, None] * gain.astype(jnp.float32)[None, :]
    payload, scales = rotate_blocks(normed, sign_in, HD)
    payload_all, scales_all = side_by_side((payload, scales), "narrow", 0, 2)
    weight_blocks = qkv_weight.reshape(payload.shape[1], HD, qkv_weight.shape[1])
    own_lists = key_cache.shape[0]
    products = jnp.einsum(
        "rbk,bkc->rbc", payload_all, weight_blocks, preferred_element_type=jnp.float32
    )
    projected = summed_on_arrival(
        jnp.einsum("rbc,rb->rc", products, scales_all.astype(jnp.float32)).astype(jnp.bfloat16),
        WIDE,
        0,
    )
    groups = key_cache.shape[1]
    grouped = projected.reshape(own_lists, groups, QG + 2, HD)
    queries = rotary(grouped[:, :, :QG, :].reshape(own_lists, groups * QG, HD), lengths)
    queries = queries.astype(jnp.bfloat16).reshape(own_lists, groups, QG, HD)
    keys_new = rotary(grouped[:, :, QG, :], lengths).astype(jnp.bfloat16)
    values_new = grouped[:, :, QG + 1, :].astype(jnp.bfloat16)
    inverse_root = 1.0 / math.sqrt(HD)
    live = jnp.arange(key_cache.shape[2], dtype=jnp.int32)[None, :] < lengths[:, None]
    live_mask = live[:, None, None, :]
    scores = (
        jnp.einsum("lgqk,lgsk->lgqs", queries, key_cache, preferred_element_type=jnp.float32)
        * inverse_root
    )
    fresh = (
        jnp.einsum("lgqk,lgk->lgq", queries, keys_new, preferred_element_type=jnp.float32)
        * inverse_root
    )
    scores = jnp.where(live_mask, scores, -1e30)
    peak = jnp.maximum(jnp.max(scores, axis=-1), fresh)
    weights = jnp.where(live_mask, jnp.exp(scores - peak[..., None]), 0.0)
    weight_new = jnp.exp(fresh - peak)
    denom_sum = jnp.sum(weights, axis=-1) + weight_new
    probs = (weights / denom_sum[..., None]).astype(jnp.bfloat16)
    prob_new = (weight_new / denom_sum).astype(jnp.bfloat16)
    attended = jnp.einsum("lgqs,lgsk->lgqk", probs, value_cache, preferred_element_type=jnp.float32)
    attended = (
        attended
        + prob_new.astype(jnp.float32)[..., None] * values_new.astype(jnp.float32)[:, :, None, :]
    )
    local_heads = groups * QG
    out_blocks, out_scale = rotate_blocks(
        attended.reshape(own_lists, local_heads * HD), sign_attn, HD
    )
    blocks_all, scale_all = side_by_side((out_blocks, out_scale), WIDE, 0, 2)
    head_weights = out_weight.reshape(local_heads, HD, out_weight.shape[1])
    products = jnp.einsum(
        "rhk,hkd->rhd", blocks_all, head_weights, preferred_element_type=jnp.float32
    )
    mixed = summed_on_arrival(
        jnp.einsum("rhd,rh->rd", products, scale_all.astype(jnp.float32)).astype(jnp.bfloat16),
        "narrow",
        0,
    )
    return (rows + mixed).astype(jnp.bfloat16)


def solution(mesh):
    split = Mesh(mesh.devices.reshape(4, 4, mesh.shape["narrow"]), ("wide_0", "wide_1", "narrow"))
    placed = (
        P("narrow", WIDE),
        P(WIDE),
        P(WIDE),
        P(WIDE, "narrow"),
        P("narrow", WIDE),
        P("narrow"),
        P(WIDE, "narrow", None, None),
        P(WIDE, "narrow", None, None),
        P(WIDE),
    )
    return jax.shard_map(
        body, mesh=split, in_specs=placed, out_specs=P("narrow", WIDE), check_vma=False
    )
```

profile of v0, /device:TPU:1, one launch (start us, length us, event | category | flops | bytes accessed | tf_op | source)
XLA Modules:
  0.0 118.0 jit_solution(16247789897836685528)
XLA Ops:
  0.0 0.7 add_convert_fusion.3
  0.7 0.7 convert_element_type.120
  1.4 0.9 fusion.37
  2.3 9.6 %psum.14 = f32[16]{0:T(128)S(1)} all-reduce(f32[16]{0:T(128)S(1)} %fusion.37), channel_id=1, replica_groups=mesh['wide_0'=4,'wide_1'=4,'narrow'=8] {'wide_0'}, use_global_device_ids=true, to_apply=%region_1.0 | all-reduce | flops 16 | bytes 128 | tf_op jit(solution)/shard_map/psum | solution.py:17
  11.8 9.7 %psum.15 = f32[16]{0:T(128)S(1)} all-reduce(f32[16]{0:T(128)S(1)} %psum.14), channel_id=1, replica_groups=mesh['wide_0'=4,'wide_1'=4,'narrow'=8] {'wide_1'}, use_global_device_ids=true, to_apply=%region_2.0 | all-reduce | flops 16 | bytes 128 | tf_op jit(solution)/shard_map/psum | solution.py:17
  21.5 0.8 fusion.40
  22.4 0.3 abs_reduce_fusion.1
  22.7 0.2 copy.28
  22.9 0.1 divide_convert_fusion.4
  23.0 18.0 %all_gather.6 = bf16[128,8,129]{2,1,0:T(8,128)(2,1)S(1)} all-gather(bf16[16,8,129]{2,1,0:T(8,128)(2,1)S(1)} %pad_maximum_fusion), channel_id=1, replica_groups=mesh['wide_0'=4,'wide_1'=4,'narrow'=8] {'narrow'}, dimensions={0}, use_global_device_ids=true | all-gather | bytes 297216 | tf_op jit(solution)/shard_map/all_gather | solution.py:24
  41.0 3.7 %convolution_bitcast_fusion = bf16[128,8,2304]{2,0,1:T(8,128)(2,1)S(1)} fusion(bf16[8,128,2304]{2,1,0:T(8,128)(2,1)} %bitcast.80, bf16[128,8,128]{2,1,0:T(8,128)(2,1)S(1)} %slice.45), kind=kOutput, calls=%fused_computation.8 | convolution fusion | flops 603979776 | bytes 9699328 | tf_op jit(solution)/shard_map/rbk,bkc->rbc/dot_general | solution.py:86
  44.8 0.0 copy-start.2
  44.8 0.0 copy-start.1
  44.8 3.4 %fusion = bf16[128,1,2304]{2,1,0:T(2,128)(2,1)S(1)} fusion(bf16[128,8,2304]{2,0,1:T(8,128)(2,1)S(1)} %convolution_bitcast_fusion, bf16[128,8,129]{2,1,0:T(8,128)(2,1)S(1)} %all_gather.6), kind=kOutput, calls=%fused_computation | convolution fusion | flops 4718592 | bytes 5570560 | tf_op jit(solution)/shard_map/rbc,rb->rc/dot_general | solution.py:90
  48.2 0.9 copy.68
  49.1 3.6 %all-to-all-start = ((bf16[16,8,2304]{2,1,0:T(8,128)(2,1)}), bf16[16,8,2304]{2,1,0:T(8,128)(2,1)S(1)}, u32[]{:S(2)}, u32[]{:S(2)}) async-start(bf16[16,8,2304]{2,1,0:T(8,128)(2,1)} %bitcast.77), calls=%async_computation | async-start | bytes 1179648 | tf_op jit(solution)/shard_map/all_to_all | solution.py:39
  52.7 0.0 copy-done.2
  52.7 0.1 iota_compare_fusion
  52.8 0.1 multiply_cosine_fusion.1
  52.9 0.0 copy-done.1
  52.9 10.8 %all-to-all-done = bf16[16,8,2304]{2,1,0:T(8,128)(2,1)S(1)} async-done(((bf16[16,8,2304]{2,1,0:T(8,128)(2,1)}), bf16[16,8,2304]{2,1,0:T(8,128)(2,1)S(1)}, u32[]{:S(2)}, u32[]{:S(2)}) %all-to-all-start) | async-done | bytes 589856 | tf_op jit(solution)/shard_map/all_to_all | solution.py:39
  63.8 0.1 convert_reduce_fusion
  63.9 0.1 fusion.63
  64.0 0.1 maximum_bitcast_fusion
  64.1 0.1 subtract_convert_fusion
  64.2 0.2 fusion.53
  64.4 5.8 %fusion.89 = (f32[8,16]{1,0:T(8,128)S(1)}, f32[8,16,4096]{2,1,0:T(8,128)S(1)}) fusion(bf16[8,1,4096,128]{3,2,1,0:T(8,128)(2,1)} %param.15, bf16[8,16,64]{2,1,0:T(8,128)(2,1)S(1)} %get-tuple-element.6, bf16[8,16,64]{2,1,0:T(8,128)(2,1)S(1)} %get-tuple-element.5, pred[8,4096]{1,0:T(8,128)(4,1)S(1)} %iota_compare_fusion), kind=kOutput, calls=%fused_computation.113 | convolution fusion | flops 135856000 | bytes 10551808 | tf_op jit(solution)/shard_map/lgqk,lgsk->lgqs/dot_general | solution.py:104
  70.2 0.6 fusion.14
  70.8 5.1 %abs_reduce_fusion = (f32[8,16]{1,0:T(8,128)S(1)}, f32[8,16,128]{2,1,0:T(8,128)S(1)}) fusion(bf16[8,1,4096,128]{3,2,1,0:T(8,128)(2,1)} %param.16, f32[8,16,4096]{2,1,0:T(8,128)S(1)} %get-tuple-element.20, f32[8,16]{1,0:T(8,128)S(1)} %get-tuple-element.8, f32[8,16]{1,0:T(8,128)S(1)} %multiply_maximum_fusion, pred[8,4096]{1,0:T(8,128)(4,1)S(1)} %iota_compare_fusion, ...), kind=kOutput, calls=%fused_computation.47 | convolution fusion | flops 141000576 | bytes 10598400 | tf_op jit(solution)/shard_map/...bk,kj->...bj/dot_general | solution.py:55
  75.9 0.1 copy.32
  76.1 0.1 divide_convert_fusion.3
  76.2 18.5 %all_gather.7 = bf16[128,16,129]{2,1,0:T(8,128)(2,1)S(1)} all-gather(bf16[8,16,129]{2,1,0:T(8,128)(2,1)S(1)} %pad_maximum_fusion.1), channel_id=1, replica_groups=mesh['wide_0'=4,'wide_1'=4,'narrow'=8] {'wide_0','wide_1'}, dimensions={0}, use_global_device_ids=true | all-gather | bytes 561408 | tf_op jit(solution)/shard_map/all_gather | solution.py:24
  94.7 0.1 slice.52
  94.8 3.4 %convolution_bitcast_fusion.1 = bf16[128,16,1024]{2,0,1:T(8,128)(2,1)S(1)} fusion(bf16[16,128,1024]{2,1,0:T(8,128)(2,1)} %bitcast.81, bf16[128,16,128]{2,1,0:T(8,128)(2,1)S(1)} %slice.52), kind=kOutput, calls=%fused_computation.11 | convolution fusion | flops 536870912 | bytes 8912896 | tf_op jit(solution)/shard_map/rhk,hkd->rhd/dot_general | solution.py:129
  98.3 0.0 copy-start
  98.3 2.6 %fusion.6 = bf16[128,1,1024]{2,1,0:T(2,128)(2,1)S(1)} fusion(bf16[128,16,1024]{2,0,1:T(8,128)(2,1)S(1)} %convolution_bitcast_fusion.1, bf16[128,16,129]{2,1,0:T(8,128)(2,1)S(1)} %all_gather.7), kind=kOutput, calls=%fused_computation.6 | convolution fusion | flops 4194304 | bytes 4980736 | tf_op jit(solution)/shard_map/rhd,rh->rd/dot_general | solution.py:133
  100.9 0.1 copy.69
  101.0 16.4 %all_to_all.10 = bf16[8,16,1024]{2,1,0:T(8,128)(2,1)S(1)} all-to-all(bf16[8,16,1024]{2,1,0:T(8,128)(2,1)S(1)} %bitcast.82), channel_id=1, replica_groups=mesh['wide_0'=4,'wide_1'=4,'narrow'=8] {'narrow'}, dimensions={0} | all-to-all | bytes 524288 | tf_op jit(solution)/shard_map/all_to_all | solution.py:39
  117.4 0.0 copy-done
  117.4 0.6 fusion.41
  (17 shorter events, 0.2 us)
Async XLA Ops:
  44.8 7.9 %copy-start.2 = (s32[8]{0:T(128)S(1)}, s32[8]{0:T(128)}, u32[]{:S(2)}) copy-start(s32[8]{0:T(128)} %param.17) | copy-start | bytes 100
  44.8 8.2 %copy-start.1 = (s32[2048]{0:T(1024)S(1)}, s32[2048]{0:T(1024)}, u32[]{:S(2)}) copy-start(s32[2048]{0:T(1024)} %param.14) | copy-start | bytes 24580
  49.1 14.7 %all-to-all-start = ((bf16[16,8,2304]{2,1,0:T(8,128)(2,1)}), bf16[16,8,2304]{2,1,0:T(8,128)(2,1)S(1)}, u32[]{:S(2)}, u32[]{:S(2)}) async-start(bf16[16,8,2304]{2,1,0:T(8,128)(2,1)} %bitcast.77), calls=%async_computation | async-start | bytes 1179648 | tf_op jit(solution)/shard_map/all_to_all | solution.py:39
  98.3 19.1 %copy-start = (bf16[16,1024]{1,0:T(8,128)(2,1)S(1)}, bf16[16,1024]{1,0:T(8,128)(2,1)}, u32[]{:S(2)}) copy-start(bf16[16,1024]{1,0:T(8,128)(2,1)} %param.9) | copy-start | bytes 98308
where the time goes:
time: 119 us; the launch traced here: 118 us
  blocking collectives  72.2 us (61%)
  matrix products  24.5 us (21%)
  waiting for transfers between devices  10.8 us (9%)
  other arithmetic  5.21 us (4%)
  starting transfers between devices  3.58 us (3%)
  local copies, waits for them, and re-layouts  1.44 us (1%)
    all_gather x2, blocking collectives, side_by_side(): lax.all_gather(both, axis, axis=dim, tiled=True)  36.5 us
    psum x2, blocking collectives, one_axis_at_a_time(): value = lax.psum(value, axis)  19.3 us
    all_to_all x1, blocking collectives, summed_on_arrival(): lax.all_to_all(tiles, axis, split_axis=0, concat_axis=0, tiled=True)  16.4 us
    all_to_all x1, waiting for transfers between devices, summed_on_arrival(): lax.all_to_all(tiles, axis, split_axis=0, concat_axis=0, tiled=True)  10.8 us
    dot_general x1, matrix products, body(): jnp.einsum('lgqk,lgsk->lgqs', queries, key_cache, preferred_element_type=...  5.79 us
    dot_general x2, matrix products, rotate_blocks(): turned = jnp.einsum('...bk,kj->...bj', blocks, hadamard(width))  5.36 us
    dot_general x1, matrix products, body(): jnp.einsum('rbk,bkc->rbc', payload_all, weight_blocks, preferred_element_...  3.71 us
    all_to_all x1, starting transfers between devices, summed_on_arrival(): lax.all_to_all(tiles, axis, split_axis=0, concat_axis=0, tiled=True)  3.58 us
  transfers between devices with their start and end apart: 1, of which 1 were waited for; matrix products, arithmetic and copies ran while one was open for 0% of the time, Pallas kernels for 0%

commit v1 on v0

--- a/solution.py
+++ b/solution.py
@@ -14,7 +14,7 @@
 
 def one_axis_at_a_time(value, axes):
     for axis in axes:
-        value = lax.psum(value, axis)
+        value = jnp.sum(jax.lax.all_gather(value, axis_name=axis), axis=0)
     return value
 
 

time: 119 us -> 123 us (1.034)
  local copies, waits for them, and re-layouts: 1.44 us -> 4.58 us
  between operations: 0.25 us -> 1.57 us
    psum x2 -> x0, blocking collectives: 19.3 us -> none  [one_axis_at_a_time(): value = lax.psum(value, axis)]
    unnamed x0 -> x2, blocking collectives: none -> 19.2 us
    unnamed x8 -> x14, local copies, waits for them, and re-layouts: 0.04 us -> 3.01 us
where the time goes in v1:
time: 123 us; the launch traced here: 122 us
  blocking collectives  72.2 us (59%)
  matrix products  24.5 us (20%)
  waiting for transfers between devices  10.8 us (9%)
  other arithmetic  5.26 us (4%)
  local copies, waits for them, and re-layouts  4.58 us (4%)
  starting transfers between devices  3.58 us (3%)
  between operations  1.57 us (1%)
    all_gather x2, blocking collectives, side_by_side(): lax.all_gather(both, axis, axis=dim, tiled=True)  36.5 us
    unnamed x2, blocking collectives  19.2 us
    all_to_all x1, blocking collectives, summed_on_arrival(): lax.all_to_all(tiles, axis, split_axis=0, concat_axis=0, tiled=True)  16.4 us
    all_to_all x1, waiting for transfers between devices, summed_on_arrival(): lax.all_to_all(tiles, axis, split_axis=0, concat_axis=0, tiled=True)  10.8 us
    dot_general x1, matrix products, body(): jnp.einsum('lgqk,lgsk->lgqs', queries, key_cache, preferred_element_type=...  5.79 us
    dot_general x2, matrix products, rotate_blocks(): turned = jnp.einsum('...bk,kj->...bj', blocks, hadamard(width))  5.36 us
    dot_general x1, matrix products, body(): jnp.einsum('rbk,bkc->rbc', payload_all, weight_blocks, preferred_element_...  3.71 us
    all_to_all x1, starting transfers between devices, summed_on_arrival(): lax.all_to_all(tiles, axis, split_axis=0, concat_axis=0, tiled=True)  3.58 us
  transfers between devices with their start and end apart: 1, of which 1 were waited for; matrix products, arithmetic and copies ran while one was open for 0% of the time, Pallas kernels for 0%

profile of v1, /device:TPU:1, one launch (start us, length us, event | category | flops | bytes accessed | tf_op | source)
XLA Modules:
  0.0 122.5 jit_solution(8889150019748252500)
XLA Ops:
  0.0 0.9 fusion.37
  0.9 1.2 %dynamic-slice = u32[1]{0:T(128)} dynamic-slice(u32[128]{0:T(128)} %constant.47, u32[]{:T(128)S(6)} %add.70), dynamic_slice_sizes={1} | dynamic-slice | bytes 12
  2.8 0.2 dynamic-update-slice
  3.0 9.5 %all-reduce = f32[64]{0:T(128)S(1)} all-reduce(f32[64]{0:T(128)S(1)} %dynamic-update-slice), channel_id=2, replica_groups=mesh['wide_0'=4,'wide_1'=4,'narrow'=8] {'wide_0'}, use_global_device_ids=true, to_apply=%add | all-reduce | flops 64 | bytes 512
  12.6 0.1 reshape.285
  12.6 1.2 %dynamic-slice.1 = u32[1]{0:T(128)} dynamic-slice(u32[128]{0:T(128)} %constant.52, u32[]{:T(128)S(6)} %add.70), dynamic_slice_sizes={1} | dynamic-slice | bytes 12
  14.6 0.2 dynamic-update-slice.1
  14.8 9.7 %all-reduce.1 = f32[64]{0:T(128)S(1)} all-reduce(f32[64]{0:T(128)S(1)} %dynamic-update-slice.1), channel_id=3, replica_groups=mesh['wide_0'=4,'wide_1'=4,'narrow'=8] {'wide_1'}, use_global_device_ids=true, to_apply=%add.1 | all-reduce | flops 64 | bytes 512
  24.5 0.1 reshape.286
  24.6 0.7 add_convert_fusion.3
  25.3 0.7 convert_element_type.120
  26.0 0.8 fusion.40
  26.9 0.3 abs_reduce_fusion.1
  27.2 0.2 copy.28
  27.3 0.1 divide_convert_fusion.4
  27.5 18.0 %all_gather.22 = bf16[128,8,129]{2,1,0:T(8,128)(2,1)S(1)} all-gather(bf16[16,8,129]{2,1,0:T(8,128)(2,1)S(1)} %pad_maximum_fusion), channel_id=1, replica_groups=mesh['wide_0'=4,'wide_1'=4,'narrow'=8] {'narrow'}, dimensions={0}, use_global_device_ids=true | all-gather | bytes 297216 | tf_op jit(solution)/shard_map/all_gather | solution.py:24
  45.5 3.7 %convolution_bitcast_fusion = bf16[128,8,2304]{2,0,1:T(8,128)(2,1)S(1)} fusion(bf16[8,128,2304]{2,1,0:T(8,128)(2,1)} %bitcast.82, bf16[128,8,128]{2,1,0:T(8,128)(2,1)S(1)} %slice.45), kind=kOutput, calls=%fused_computation.8 | convolution fusion | flops 603979776 | bytes 9699328 | tf_op jit(solution)/shard_map/rbk,bkc->rbc/dot_general | solution.py:86
  49.2 0.0 copy-start.2
  49.2 0.0 copy-start.1
  49.2 3.4 %fusion = bf16[128,1,2304]{2,1,0:T(2,128)(2,1)S(1)} fusion(bf16[128,8,2304]{2,0,1:T(8,128)(2,1)S(1)} %convolution_bitcast_fusion, bf16[128,8,129]{2,1,0:T(8,128)(2,1)S(1)} %all_gather.22), kind=kOutput, calls=%fused_computation | convolution fusion | flops 4718592 | bytes 5570560 | tf_op jit(solution)/shard_map/rbc,rb->rc/dot_general | solution.py:90
  52.7 0.9 copy.68
  53.6 3.6 %all-to-all-start = ((bf16[16,8,2304]{2,1,0:T(8,128)(2,1)}), bf16[16,8,2304]{2,1,0:T(8,128)(2,1)S(1)}, u32[]{:S(2)}, u32[]{:S(2)}) async-start(bf16[16,8,2304]{2,1,0:T(8,128)(2,1)} %bitcast.79), calls=%async_computation | async-start | bytes 1179648 | tf_op jit(solution)/shard_map/all_to_all | solution.py:39
  57.1 0.0 copy-done.2
  57.2 0.1 iota_compare_fusion
  57.3 0.1 multiply_cosine_fusion.1
  57.4 0.0 copy-done.1
  57.4 10.8 %all-to-all-done = bf16[16,8,2304]{2,1,0:T(8,128)(2,1)S(1)} async-done(((bf16[16,8,2304]{2,1,0:T(8,128)(2,1)}), bf16[16,8,2304]{2,1,0:T(8,128)(2,1)S(1)}, u32[]{:S(2)}, u32[]{:S(2)}) %all-to-all-start) | async-done | bytes 589856 | tf_op jit(solution)/shard_map/all_to_all | solution.py:39
  68.2 0.1 convert_reduce_fusion
  68.3 0.1 fusion.63
  68.5 0.1 maximum_bitcast_fusion
  68.5 0.1 subtract_convert_fusion
  68.6 0.2 fusion.53
  68.8 5.8 %fusion.89 = (f32[8,16]{1,0:T(8,128)S(1)}, f32[8,16,4096]{2,1,0:T(8,128)S(1)}) fusion(bf16[8,1,4096,128]{3,2,1,0:T(8,128)(2,1)} %param.15, bf16[8,16,64]{2,1,0:T(8,128)(2,1)S(1)} %get-tuple-element.6, bf16[8,16,64]{2,1,0:T(8,128)(2,1)S(1)} %get-tuple-element.5, pred[8,4096]{1,0:T(8,128)(4,1)S(1)} %iota_compare_fusion), kind=kOutput, calls=%fused_computation.113 | convolution fusion | flops 135856000 | bytes 10551808 | tf_op jit(solution)/shard_map/lgqk,lgsk->lgqs/dot_general | solution.py:104
  74.6 0.6 fusion.14
  75.3 5.1 %abs_reduce_fusion = (f32[8,16]{1,0:T(8,128)S(1)}, f32[8,16,128]{2,1,0:T(8,128)S(1)}) fusion(bf16[8,1,4096,128]{3,2,1,0:T(8,128)(2,1)} %param.16, f32[8,16,4096]{2,1,0:T(8,128)S(1)} %get-tuple-element.20, f32[8,16]{1,0:T(8,128)S(1)} %get-tuple-element.8, f32[8,16]{1,0:T(8,128)S(1)} %multiply_maximum_fusion, pred[8,4096]{1,0:T(8,128)(4,1)S(1)} %iota_compare_fusion, ...), kind=kOutput, calls=%fused_computation.47 | convolution fusion | flops 141000576 | bytes 10598400 | tf_op jit(solution)/shard_map/...bk,kj->...bj/dot_general | solution.py:55
  80.4 0.1 copy.32
  80.5 0.1 divide_convert_fusion.3
  80.7 18.5 %all_gather.23 = bf16[128,16,129]{2,1,0:T(8,128)(2,1)S(1)} all-gather(bf16[8,16,129]{2,1,0:T(8,128)(2,1)S(1)} %pad_maximum_fusion.1), channel_id=1, replica_groups=mesh['wide_0'=4,'wide_1'=4,'narrow'=8] {'wide_0','wide_1'}, dimensions={0}, use_global_device_ids=true | all-gather | bytes 561408 | tf_op jit(solution)/shard_map/all_gather | solution.py:24
  99.2 0.1 slice.52
  99.3 3.4 %convolution_bitcast_fusion.1 = bf16[128,16,1024]{2,0,1:T(8,128)(2,1)S(1)} fusion(bf16[16,128,1024]{2,1,0:T(8,128)(2,1)} %bitcast.83, bf16[128,16,128]{2,1,0:T(8,128)(2,1)S(1)} %slice.52), kind=kOutput, calls=%fused_computation.11 | convolution fusion | flops 536870912 | bytes 8912896 | tf_op jit(solution)/shard_map/rhk,hkd->rhd/dot_general | solution.py:129
  102.7 0.0 copy-start
  102.7 2.6 %fusion.6 = bf16[128,1,1024]{2,1,0:T(2,128)(2,1)S(1)} fusion(bf16[128,16,1024]{2,0,1:T(8,128)(2,1)S(1)} %convolution_bitcast_fusion.1, bf16[128,16,129]{2,1,0:T(8,128)(2,1)S(1)} %all_gather.23), kind=kOutput, calls=%fused_computation.6 | convolution fusion | flops 4194304 | bytes 4980736 | tf_op jit(solution)/shard_map/rhd,rh->rd/dot_general | solution.py:133
  105.3 0.1 copy.69
  105.4 16.4 %all_to_all.10 = bf16[8,16,1024]{2,1,0:T(8,128)(2,1)S(1)} all-to-all(bf16[8,16,1024]{2,1,0:T(8,128)(2,1)S(1)} %bitcast.84), channel_id=1, replica_groups=mesh['wide_0'=4,'wide_1'=4,'narrow'=8] {'narrow'}, dimensions={0} | all-to-all | bytes 524288 | tf_op jit(solution)/shard_map/all_to_all | solution.py:39
  121.8 0.0 copy-done
  121.8 0.6 fusion.41
  (21 shorter events, 0.2 us)
Async XLA Ops:
  49.2 7.9 %copy-start.2 = (s32[8]{0:T(128)S(1)}, s32[8]{0:T(128)}, u32[]{:S(2)}) copy-start(s32[8]{0:T(128)} %param.17) | copy-start | bytes 100
  49.2 8.2 %copy-start.1 = (s32[2048]{0:T(1024)S(1)}, s32[2048]{0:T(1024)}, u32[]{:S(2)}) copy-start(s32[2048]{0:T(1024)} %param.14) | copy-start | bytes 24580
  53.6 14.7 %all-to-all-start = ((bf16[16,8,2304]{2,1,0:T(8,128)(2,1)}), bf16[16,8,2304]{2,1,0:T(8,128)(2,1)S(1)}, u32[]{:S(2)}, u32[]{:S(2)}) async-start(bf16[16,8,2304]{2,1,0:T(8,128)(2,1)} %bitcast.79), calls=%async_computation | async-start | bytes 1179648 | tf_op jit(solution)/shard_map/all_to_all | solution.py:39
  102.7 19.1 %copy-start = (bf16[16,1024]{1,0:T(8,128)(2,1)S(1)}, bf16[16,1024]{1,0:T(8,128)(2,1)}, u32[]{:S(2)}) copy-start(bf16[16,1024]{1,0:T(8,128)(2,1)} %param.9) | copy-start | bytes 98308
